TPU v7x, 32 devices: a whole 2x2x4 slice. The times are simulated.
32 devices in a mesh: parts: 2 (over x), wide: 16 (over z, y, core).
Axes of the slice: x: 2, y: 2, z: 4, core: 2. Of those that a mesh axis runs over, the one named last changes fastest.
Arguments:
- tokens: bfloat16 [384, 7168], P(('parts', 'wide')), parts along dimension 0, may hold values from -6 to 6
- expert_ids: int32 [384, 8], P(('parts', 'wide')), parts along dimension 0, may hold values from 0 to 15, as said below
- gates: float32 [384, 8], P(('parts', 'wide')), parts along dimension 0, may hold values from 0.1 to 1
- w_gate: bfloat16 [2, 7168, 8192], P(None, None, 'wide'), may hold values from -0.0625 to 0.0625
- w_up: bfloat16 [2, 7168, 8192], P(None, None, 'wide'), may hold values from -0.0625 to 0.0625
- w_down: bfloat16 [2, 8192, 7168], P(None, 'wide'), may hold values from -0.1875 to 0.1875
Outputs:
- moe_out: bfloat16 [384, 7168], P(('parts', 'wide')), parts along dimension 0
There are 2 independent parts, one for each index of `parts`. A program takes and returns all parts, laid end to end along the dimension named above; an argument that names none is the same for every part. Nothing has to cross between parts.
Inputs may be any that keep to these rules, and one draw needn't show every extreme that they name: `expert_ids`: each row names the 2 experts g * 2 to g * 2 + 1 of each of 4 different groups g, in any order; in each part one group is named by every row.
All inputs are finite; a program needn't handle non-finite values.
Results may differ from a plain program's by a relative error of at most 0.0064.
Values may be sent and summed in bfloat16 or wider, within the bound.
A program may use at most 128 MiB of HBM per device.

v0:
```python
import jax
import jax.numpy as jnp
from jax import lax
from jax.sharding import PartitionSpec as P

GROUPS = 8
EXP_G = 2


def partner(block, axis, bit):
    count = lax.axis_size(axis)
    route = []
    for low in range(count):
        high = low | 1 << bit
        if high != low and high < count:
            route += [(low, high), (high, low)]
    return lax.ppermute(block, axis, route)


def route_table(expert_ids, gates):
    token_count = expert_ids.shape[0]
    catalog = jnp.arange(GROUPS * EXP_G, dtype=jnp.int32)
    picked = expert_ids[:, :, None] == catalog[None, None, :]
    weight_sum = jnp.sum(jnp.where(picked, gates[:, :, None], 0.0), axis=1)
    return weight_sum.astype(jnp.bfloat16).reshape(token_count, GROUPS, EXP_G)


def selection(expert_ids, wide_count, group_size, slot_count):
    token_count = expert_ids.shape[0]
    group_ids = jnp.arange(GROUPS, dtype=jnp.int32)
    member = jnp.any((expert_ids // EXP_G)[:, :, None] == group_ids[None, None, :], axis=1)
    position = jnp.cumsum(member.astype(jnp.int32), axis=0) - 1
    target = jnp.arange(wide_count, dtype=jnp.int32)
    target_group = (target // group_size)[:, None] == group_ids[None, :]
    target_rank = target % group_size
    member_dest = jnp.any(target_group[:, :, None] & member.T[None, :, :], axis=1)
    position_dest = jnp.sum(jnp.where(target_group[:, :, None], position.T[None, :, :], 0), axis=1)
    stride = token_count // slot_count
    wanted = (
        jnp.arange(slot_count, dtype=jnp.int32)[None, :] * stride + (target_rank % stride)[:, None]
    )
    chosen = member_dest[:, None, :] & (position_dest[:, None, :] == wanted[:, :, None])
    return (chosen, target_group)


def pack(tokens, route_weight, chosen, target_group):
    wide_count, slot_count, token_count = chosen.shape
    pick_table = chosen.astype(jnp.bfloat16).reshape(wide_count * slot_count, token_count)
    packed = jnp.dot(pick_table, tokens, preferred_element_type=jnp.float32).astype(jnp.bfloat16)
    packed = packed.reshape(wide_count, slot_count, tokens.shape[1])
    route_dest = jnp.einsum(
        "dg,tgj->dtj",
        target_group.astype(jnp.float32),
        route_weight.astype(jnp.float32),
        precision=lax.Precision.HIGHEST,
    )
    scaled = jnp.einsum(
        "dst,dtj->dsj", chosen.astype(jnp.float32), route_dest, precision=lax.Precision.HIGHEST
    )
    return (packed, scaled.astype(jnp.bfloat16))


def expert_block(inputs, scales, w_gate, w_up, w_down):
    summed = jnp.zeros((inputs.shape[0], w_down.shape[2]), jnp.float32)
    for expert in range(EXP_G):
        gate_value = jnp.dot(inputs, w_gate[expert], preferred_element_type=jnp.float32)
        lifted = jnp.dot(inputs, w_up[expert], preferred_element_type=jnp.float32)
        hidden = (jax.nn.silu(gate_value) * lifted).astype(jnp.bfloat16)
        summed = summed + scales[:, expert : expert + 1].astype(jnp.float32) * jnp.dot(
            hidden, w_down[expert], preferred_element_type=jnp.float32
        )
    return summed.astype(jnp.bfloat16)


def local(tokens, expert_ids, gates, w_gate, w_up, w_down):
    wide_count = lax.axis_size("wide")
    group_size = wide_count // GROUPS
    token_count = tokens.shape[0]
    model_width = tokens.shape[1]
    route_weight = route_table(expert_ids, gates)
    slot_count = token_count // group_size
    chosen, target_group = selection(expert_ids, wide_count, group_size, slot_count)
    packed, scaled = pack(tokens, route_weight, chosen, target_group)
    arrived, arrived_scale = (
        lax.all_to_all(packed, "wide", split_axis=0, concat_axis=0, tiled=True),
        lax.all_to_all(scaled, "wide", split_axis=0, concat_axis=0, tiled=True),
    )
    my_rank = lax.axis_index("wide") % group_size
    levels = group_size.bit_length() - 1
    held_rows = arrived[None]
    held_scale = arrived_scale[None]
    for level_index in range(levels):
        partner_rows, partner_scale = partner((held_rows, held_scale), "wide", level_index)
        upper_half = my_rank // (1 << level_index) % 2 == 1
        held_rows = jnp.concatenate(
            [
                jnp.where(upper_half, partner_rows, held_rows),
                jnp.where(upper_half, held_rows, partner_rows),
            ],
            0,
        )
        held_scale = jnp.concatenate(
            [
                jnp.where(upper_half, partner_scale, held_scale),
                jnp.where(upper_half, held_scale, partner_scale),
            ],
            0,
        )
    partial_value = expert_block(
        held_rows.reshape(-1, model_width), held_scale.reshape(-1, EXP_G), w_gate, w_up, w_down
    )
    partial_value = partial_value.reshape(group_size, wide_count, slot_count, model_width)
    returned = lax.all_to_all(partial_value, "wide", split_axis=1, concat_axis=1, tiled=True)
    chosen_grouped = chosen.reshape(GROUPS, group_size, slot_count, token_count).transpose(
        1, 0, 2, 3
    )
    pick_rows = jnp.broadcast_to(
        chosen_grouped[:, :, None], (group_size, GROUPS, group_size, slot_count, token_count)
    )
    pick_table = pick_rows.reshape(group_size * wide_count * slot_count, token_count).T.astype(
        jnp.bfloat16
    )
    output = jnp.dot(
        pick_table, returned.reshape(-1, model_width), preferred_element_type=jnp.float32
    )
    return output.astype(jnp.bfloat16)


def solution(mesh):
    return jax.shard_map(
        local,
        mesh=mesh,
        in_specs=(
            P(("parts", "wide"), None),
            P(("parts", "wide"), None),
            P(("parts", "wide"), None),
            P(None, None, "wide"),
            P(None, None, "wide"),
            P(None, "wide", None),
        ),
        out_specs=P(("parts", "wide"), None),
        check_vma=False,
    )
```

profile of v0, /device:TPU:15, one launch (start us, length us, event | category | flops | bytes accessed | tf_op | source)
XLA Modules:
  0.0 191.6 jit_solution(12496329950907122249)
XLA Ops:
  0.0 0.8 add_select_fusion
  2.7 1.5 reshape.140
  4.2 6.5 %all-to-all-start.1 = ((bf16[16,6,7168]{2,1,0:T(8,128)(2,1)}), bf16[16,6,7168]{2,1,0:T(8,128)(2,1)S(1)}, u32[]{:S(2)}, u32[]{:S(2)}) async-start(bf16[16,6,7168]{2,1,0:T(8,128)(2,1)} %reshape.140), calls=%async_computation.1 | async-start | bytes 3670016 | tf_op jit(solution)/shard_map/all_to_all | solution.py:85
  11.1 41.4 %all-to-all-done.1 = bf16[16,6,7168]{2,1,0:T(8,128)(2,1)S(1)} async-done(((bf16[16,6,7168]{2,1,0:T(8,128)(2,1)}), bf16[16,6,7168]{2,1,0:T(8,128)(2,1)S(1)}, u32[]{:S(2)}, u32[]{:S(2)}) %all-to-all-start.1) | async-done | bytes 1376288 | tf_op jit(solution)/shard_map/all_to_all | solution.py:85
  52.5 1.9 copy.64
  54.9 0.8 convolution_convert_fusion.2
  55.7 5.1 %all-to-all-start = ((bf16[16,6,2]{1,2,0:T(2,128)(2,1)}), bf16[16,6,2]{1,2,0:T(2,128)(2,1)S(1)}, u32[]{:S(2)}, u32[]{:S(2)}) async-start(bf16[16,6,2]{1,2,0:T(2,128)(2,1)} %convolution_convert_fusion.2), calls=%async_computation | async-start | bytes 16384 | tf_op jit(solution)/shard_map/all_to_all | solution.py:86
  60.7 3.8 %all-to-all-done = bf16[16,6,2]{1,2,0:T(2,128)(2,1)S(1)} async-done(((bf16[16,6,2]{1,2,0:T(2,128)(2,1)}), bf16[16,6,2]{1,2,0:T(2,128)(2,1)S(1)}, u32[]{:S(2)}, u32[]{:S(2)}) %all-to-all-start) | async-done | bytes 416 | tf_op jit(solution)/shard_map/all_to_all | solution.py:86
  64.5 0.7 collective-permute-start
  65.2 0.8 collective-permute-done
  66.2 1.7 copy_select_fusion.1
  67.9 2.6 %pad_maximum_fusion = bf16[2,16,6,7168]{3,2,1,0:T(8,128)(2,1)} fusion(bf16[1,16,6,7168]{3,2,1,0:T(8,128)(2,1)S(1)} %get-tuple-element.6, bf16[1,16,6,7168]{3,2,1,0:T(8,128)(2,1)S(1)} %get-tuple-element.5), kind=kLoop, calls=%fused_computation.22 | loop fusion | flops 1376256 | bytes 5505024 | tf_op jit(solution)/shard_map/concatenate | solution.py:95
  70.5 3.2 %reshape.141 = bf16[192,7168]{1,0:T(8,128)(2,1)S(1)} reshape(bf16[2,16,6,7168]{3,2,1,0:T(8,128)(2,1)} %pad_maximum_fusion) | data formatting | bytes 5505024 | tf_op jit(solution)/shard_map/reshape | solution.py:110
  73.7 5.5 %fusion.3 = f32[192,512]{1,0:T(8,128)} fusion(bf16[192,7168]{1,0:T(8,128)(2,1)S(1)} %reshape.141, bf16[2,7168,512]{2,1,0:T(8,128)(2,1)} %param.10), kind=kOutput, calls=%fused_computation.7 | convolution fusion | flops 1409286144 | bytes 10485760 | tf_op jit(solution)/shard_map/dot_general | solution.py:67
  79.2 4.7 %fusion.8 = f32[192,512]{1,0:T(8,128)S(1)} fusion(bf16[192,7168]{1,0:T(8,128)(2,1)S(1)} %reshape.141, bf16[2,7168,512]{2,1,0:T(8,128)(2,1)} %param.10), kind=kOutput, calls=%fused_computation.12 | convolution fusion | flops 1409286144 | bytes 10485760 | tf_op jit(solution)/shard_map/dot_general | solution.py:67
  83.9 10.9 %convolution_multiply_fusion = f32[192,7168]{1,0:T(8,128)} fusion(bf16[2,512,7168]{2,1,0:T(8,128)(2,1)} %param.11, f32[192]{0:T(256)S(1)} %bitcast.69, f32[192,512]{1,0:T(8,128)} %fusion.3, bf16[192,7168]{1,0:T(8,128)(2,1)S(1)} %reshape.141, bf16[2,7168,512]{2,1,0:T(8,128)(2,1)} %param.9), kind=kOutput, calls=%fused_computation | convolution fusion | flops 2820538368 | bytes 23331584 | tf_op jit(solution)/shard_map/dot_general | solution.py:69
  94.8 11.4 %fusion.1 = bf16[192,7168]{1,0:T(8,128)(2,1)} fusion(f32[192,7168]{1,0:T(8,128)} %convolution_multiply_fusion, bf16[2,512,7168]{2,1,0:T(8,128)(2,1)} %param.11, f32[192]{0:T(256)S(1)} %bitcast.68, f32[192,512]{1,0:T(8,128)S(1)} %fusion.8, bf16[192,7168]{1,0:T(8,128)(2,1)S(1)} %reshape.141, bf16[2,7168,512]{2,1,0:T(8,128)(2,1)} %param.9), kind=kOutput, calls=%fused_computation.3 | convolution fusion | flops 2823290880 | bytes 26084096 | tf_op jit(solution)/shard_map/dot_general | solution.py:69
  106.2 4.6 %reshape.142 = bf16[2,16,6,7168]{3,2,1,0:T(8,128)(2,1)} reshape(bf16[192,7168]{1,0:T(8,128)(2,1)} %fusion.1) | data formatting | bytes 5505024 | tf_op jit(solution)/shard_map/reshape | solution.py:112
  110.8 6.4 %copy.67 = bf16[2,16,6,7168]{3,0,2,1:T(2,128)(2,1)} copy(bf16[2,16,6,7168]{3,2,1,0:T(8,128)(2,1)} %reshape.142) | data formatting | bytes 5505024 | tf_op jit(solution)/shard_map/reshape | solution.py:112
  117.2 5.9 %all-to-all-start.2 = ((bf16[2,16,6,7168]{3,0,2,1:T(2,128)(2,1)}), bf16[2,16,6,7168]{3,0,2,1:T(2,128)(2,1)S(1)}, u32[]{:S(2)}, u32[]{:S(2)}) async-start(bf16[2,16,6,7168]{3,0,2,1:T(2,128)(2,1)} %copy.67), calls=%async_computation.2 | async-start | bytes 5505024 | tf_op jit(solution)/shard_map/all_to_all | solution.py:113
  123.6 61.0 %all-to-all-done.2 = bf16[2,16,6,7168]{3,0,2,1:T(2,128)(2,1)S(1)} async-done(((bf16[2,16,6,7168]{3,0,2,1:T(2,128)(2,1)}), bf16[2,16,6,7168]{3,0,2,1:T(2,128)(2,1)S(1)}, u32[]{:S(2)}, u32[]{:S(2)}) %all-to-all-start.2) | async-done | bytes 2752544 | tf_op jit(solution)/shard_map/all_to_all | solution.py:113
  184.6 2.5 %copy.68 = bf16[2,16,6,7168]{3,2,1,0:T(8,128)(2,1)} copy(bf16[2,16,6,7168]{3,0,2,1:T(2,128)(2,1)S(1)} %all-to-all-done.2) | data formatting | bytes 5505024 | tf_op jit(solution)/shard_map/all_to_all | solution.py:113
  187.2 3.2 %reshape.143 = bf16[192,7168]{1,0:T(8,128)(2,1)S(1)} reshape(bf16[2,16,6,7168]{3,2,1,0:T(8,128)(2,1)} %copy.68) | data formatting | bytes 5505024 | tf_op jit(solution)/shard_map/reshape | solution.py:124
  190.4 1.2 convolution_convert_fusion.1
  (54 shorter events, 3.3 us)
Async XLA Ops:
  0.0 2.1 %copy-start = (bf16[12,7168]{1,0:T(8,128)(2,1)S(1)}, bf16[12,7168]{1,0:T(8,128)(2,1)}, u32[]{:S(2)}) copy-start(bf16[12,7168]{1,0:T(8,128)(2,1)} %param.6) | copy-start | bytes 516100
  2.6 8.1 %copy-start.2 = (s32[12,8]{0,1:T(8,128)S(1)}, s32[12,8]{0,1:T(8,128)}, u32[]{:S(2)}) copy-start(s32[12,8]{0,1:T(8,128)} %param.7) | copy-start | bytes 1156
  2.7 8.2 %copy-start.3 = (f32[12,8]{0,1:T(8,128)S(1)}, f32[12,8]{0,1:T(8,128)}, u32[]{:S(2)}) copy-start(f32[12,8]{0,1:T(8,128)} %param.8) | copy-start | bytes 1156
  4.2 48.3 %all-to-all-start.1 = ((bf16[16,6,7168]{2,1,0:T(8,128)(2,1)}), bf16[16,6,7168]{2,1,0:T(8,128)(2,1)S(1)}, u32[]{:S(2)}, u32[]{:S(2)}) async-start(bf16[16,6,7168]{2,1,0:T(8,128)(2,1)} %reshape.140), calls=%async_computation.1 | async-start | bytes 3670016 | tf_op jit(solution)/shard_map/all_to_all | solution.py:85
  54.4 11.8 %collective-permute-start.1 = (bf16[1,16,6,7168]{3,1,2,0:T(8,128)(2,1)}, bf16[1,16,6,7168]{3,1,2,0:T(8,128)(2,1)S(1)}, u32[]{:S(2)}, u32[]{:S(2)}) collective-permute-start(bf16[1,16,6,7168]{3,1,2,0:T(8,128)(2,1)} %copy.64), channel_id=1, source_target_pairs={{0,1},{1,0},{2,3},{3,2},{4,5},{5,4},{6,7},{7,6},{8,9},{9,8},{10,11... | collective-permute-start | bytes 4128776 | tf_op jit(solution)/shard_map/ppermute | solution.py:17
  55.7 8.9 %all-to-all-start = ((bf16[16,6,2]{1,2,0:T(2,128)(2,1)}), bf16[16,6,2]{1,2,0:T(2,128)(2,1)S(1)}, u32[]{:S(2)}, u32[]{:S(2)}) async-start(bf16[16,6,2]{1,2,0:T(2,128)(2,1)} %convolution_convert_fusion.2), calls=%async_computation | async-start | bytes 16384 | tf_op jit(solution)/shard_map/all_to_all | solution.py:86
  64.5 1.5 collective-permute-start
  117.2 67.4 %all-to-all-start.2 = ((bf16[2,16,6,7168]{3,0,2,1:T(2,128)(2,1)}), bf16[2,16,6,7168]{3,0,2,1:T(2,128)(2,1)S(1)}, u32[]{:S(2)}, u32[]{:S(2)}) async-start(bf16[2,16,6,7168]{3,0,2,1:T(2,128)(2,1)} %copy.67), calls=%async_computation.2 | async-start | bytes 5505024 | tf_op jit(solution)/shard_map/all_to_all | solution.py:113
  184.6 7.0 %copy-start.1 = (bf16[12,7168]{1,0:T(8,128)(2,1)S(1)}, bf16[12,7168]{1,0:T(8,128)(2,1)}, u32[]{:S(2)}) copy-start(bf16[12,7168]{1,0:T(8,128)(2,1)} %param.6) | copy-start | bytes 516100
where the time goes:
time: 192 us
  waiting for transfers between devices  107 us (56%)
  matrix products  35.2 us (18%)
  local copies, waits for them, and re-layouts  24.9 us (13%)
  starting transfers between devices  18.3 us (10%)
  other arithmetic  5.96 us (3%)
    all_to_all x1, waiting for transfers between devices, local(): lax.all_to_all(partial_value, 'wide', split_axis=1, concat_axis=1, tiled=...  61 us
    all_to_all x1, waiting for transfers between devices, local(): lax.all_to_all(packed, 'wide', split_axis=0, concat_axis=0, tiled=True)  41.4 us
    dot_general x2, matrix products, expert_block(): jnp.dot(hidden, w_down[expert], preferred_element_type=jnp.float32)  22.3 us
    reshape x2, local copies, waits for them, and re-layouts, local(): partial_value.reshape(group_size, wide_count, slot_count, model_width)  11 us
    dot_general x2, matrix products, expert_block(): lifted = jnp.dot(inputs, w_up[expert], preferred_element_type=jnp.float32)  10.1 us
    all_to_all x1, starting transfers between devices, local(): lax.all_to_all(packed, 'wide', split_axis=0, concat_axis=0, tiled=True)  6.52 us
    all_to_all x1, starting transfers between devices, local(): lax.all_to_all(partial_value, 'wide', split_axis=1, concat_axis=1, tiled=...  5.92 us
    all_to_all x1, starting transfers between devices, local(): lax.all_to_all(scaled, 'wide', split_axis=0, concat_axis=0, tiled=True)  5.06 us
  transfers between devices with their start and end apart: 5, of which 4 were waited for; matrix products, arithmetic and copies ran while one was open for 1% of the time, Pallas kernels for 0%

commit v1 on v0

--- a/solution.py
+++ b/solution.py
@@ -110,7 +110,12 @@
         held_rows.reshape(-1, model_width), held_scale.reshape(-1, EXP_G), w_gate, w_up, w_down
     )
     partial_value = partial_value.reshape(group_size, wide_count, slot_count, model_width)
-    returned = lax.all_to_all(partial_value, "wide", split_axis=1, concat_axis=1, tiled=True)
+    returned = jnp.concatenate(
+        lax.all_to_all(
+            jnp.stack(jnp.split(partial_value, lax.axis_size("wide"), axis=1)), "wide", 0, 0
+        ),
+        axis=1,
+    )
     chosen_grouped = chosen.reshape(GROUPS, group_size, slot_count, token_count).transpose(
         1, 0, 2, 3
     )

time: 192 us -> 206 us (1.073)
  local copies, waits for them, and re-layouts: 24.9 us -> 38.1 us
    unnamed x10 -> x25, local copies, waits for them, and re-layouts: 0.19 us -> 14.5 us
    another operation x0 -> x3, local copies, waits for them, and re-layouts: none -> 8.56 us  [the longest x2 5.34 us: local(): jnp.stack(jnp.split(partial_value, lax.axis_size('wide'), axis=1))]
    reshape x2 -> x1, local copies, waits for them, and re-layouts: 11 us -> 4.61 us  [local(): partial_value.reshape(group_size, wide_count, slot_count, model_width)]
    all_to_all x1 -> x0, local copies, waits for them, and re-layouts: 2.53 us -> none  [local(): lax.all_to_all(partial_value, 'wide', split_axis=1, concat_axis=1, tiled=...]
where the time goes in v1:
time: 206 us; the launch traced here: 205 us
  waiting for transfers between devices  107 us (52%)
  local copies, waits for them, and re-layouts  38.1 us (18%)
  matrix products  35.2 us (17%)
  starting transfers between devices  18.3 us (9%)
  other arithmetic  5.96 us (3%)
    all_to_all x1, waiting for transfers between devices, local(): lax.all_to_all(jnp.stack(jnp.split(partial_value, lax.axis_size('wide'),...  61 us
    all_to_all x1, waiting for transfers between devices, local(): lax.all_to_all(packed, 'wide', split_axis=0, concat_axis=0, tiled=True)  41.4 us
    dot_general x2, matrix products, expert_block(): jnp.dot(hidden, w_down[expert], preferred_element_type=jnp.float32)  22.3 us
    unnamed x25, local copies, waits for them, and re-layouts  14.5 us
    dot_general x2, matrix products, expert_block(): lifted = jnp.dot(inputs, w_up[expert], preferred_element_type=jnp.float32)  10.1 us
    all_to_all x1, starting transfers between devices, local(): lax.all_to_all(packed, 'wide', split_axis=0, concat_axis=0, tiled=True)  6.52 us
    all_to_all x1, starting transfers between devices, local(): lax.all_to_all(jnp.stack(jnp.split(partial_value, lax.axis_size('wide'),...  5.92 us
    another operation x2, local copies, waits for them, and re-layouts, local(): jnp.stack(jnp.split(partial_value, lax.axis_size('wide'), axis=1))  5.34 us
  transfers between devices with their start and end apart: 5, of which 4 were waited for; matrix products, arithmetic and copies ran while one was open for 1% of the time, Pallas kernels for 0%

profile of v1, /device:TPU:15, one launch (start us, length us, event | category | flops | bytes accessed | tf_op | source)
XLA Modules:
  0.0 204.9 jit_solution(1989519738851622746)
XLA Ops:
  2.7 1.5 reshape.140
  4.2 6.5 %all-to-all-start.1 = ((bf16[16,6,7168]{2,1,0:T(8,128)(2,1)}), bf16[16,6,7168]{2,1,0:T(8,128)(2,1)S(1)}, u32[]{:S(2)}, u32[]{:S(2)}) async-start(bf16[16,6,7168]{2,1,0:T(8,128)(2,1)} %reshape.140), calls=%async_computation.1 | async-start | bytes 3670016 | tf_op jit(solution)/shard_map/all_to_all | solution.py:85
  11.1 41.4 %all-to-all-done.1 = bf16[16,6,7168]{2,1,0:T(8,128)(2,1)S(1)} async-done(((bf16[16,6,7168]{2,1,0:T(8,128)(2,1)}), bf16[16,6,7168]{2,1,0:T(8,128)(2,1)S(1)}, u32[]{:S(2)}, u32[]{:S(2)}) %all-to-all-start.1) | async-done | bytes 1376288 | tf_op jit(solution)/shard_map/all_to_all | solution.py:85
  52.5 1.9 copy.126
  55.7 5.1 %all-to-all-start = ((bf16[16,6,2]{1,2,0:T(2,128)(2,1)}), bf16[16,6,2]{1,2,0:T(2,128)(2,1)S(1)}, u32[]{:S(2)}, u32[]{:S(2)}) async-start(bf16[16,6,2]{1,2,0:T(2,128)(2,1)} %convolution_convert_fusion.2), calls=%async_computation | async-start | bytes 16384 | tf_op jit(solution)/shard_map/all_to_all | solution.py:86
  60.7 3.8 %all-to-all-done = bf16[16,6,2]{1,2,0:T(2,128)(2,1)S(1)} async-done(((bf16[16,6,2]{1,2,0:T(2,128)(2,1)}), bf16[16,6,2]{1,2,0:T(2,128)(2,1)S(1)}, u32[]{:S(2)}, u32[]{:S(2)}) %all-to-all-start) | async-done | bytes 416 | tf_op jit(solution)/shard_map/all_to_all | solution.py:86
  66.2 1.7 copy_select_fusion.1
  67.9 2.6 %pad_maximum_fusion = bf16[2,16,6,7168]{3,2,1,0:T(8,128)(2,1)} fusion(bf16[1,16,6,7168]{3,2,1,0:T(8,128)(2,1)S(1)} %get-tuple-element.6, bf16[1,16,6,7168]{3,2,1,0:T(8,128)(2,1)S(1)} %get-tuple-element.5), kind=kLoop, calls=%fused_computation.22 | loop fusion | flops 1376256 | bytes 5505024 | tf_op jit(solution)/shard_map/concatenate | solution.py:95
  70.5 3.2 %reshape.141 = bf16[192,7168]{1,0:T(8,128)(2,1)S(1)} reshape(bf16[2,16,6,7168]{3,2,1,0:T(8,128)(2,1)} %pad_maximum_fusion) | data formatting | bytes 5505024 | tf_op jit(solution)/shard_map/reshape | solution.py:110
  73.7 5.5 %fusion.3 = f32[192,512]{1,0:T(8,128)} fusion(bf16[192,7168]{1,0:T(8,128)(2,1)S(1)} %reshape.141, bf16[2,7168,512]{2,1,0:T(8,128)(2,1)} %param.10), kind=kOutput, calls=%fused_computation.7 | convolution fusion | flops 1409286144 | bytes 10485760 | tf_op jit(solution)/shard_map/dot_general | solution.py:67
  79.2 4.7 %fusion.8 = f32[192,512]{1,0:T(8,128)S(1)} fusion(bf16[192,7168]{1,0:T(8,128)(2,1)S(1)} %reshape.141, bf16[2,7168,512]{2,1,0:T(8,128)(2,1)} %param.10), kind=kOutput, calls=%fused_computation.12 | convolution fusion | flops 1409286144 | bytes 10485760 | tf_op jit(solution)/shard_map/dot_general | solution.py:67
  83.9 10.9 %convolution_multiply_fusion = f32[192,7168]{1,0:T(8,128)} fusion(bf16[2,512,7168]{2,1,0:T(8,128)(2,1)} %param.11, f32[192]{0:T(256)S(1)} %bitcast.167, f32[192,512]{1,0:T(8,128)} %fusion.3, bf16[192,7168]{1,0:T(8,128)(2,1)S(1)} %reshape.141, bf16[2,7168,512]{2,1,0:T(8,128)(2,1)} %param.9), kind=kOutput, calls=%fused_computation | convolution fusion | flops 2820538368 | bytes 23331584 | tf_op jit(solution)/shard_map/dot_general | solution.py:69
  94.8 11.4 %fusion.1 = bf16[192,7168]{1,0:T(8,128)(2,1)} fusion(f32[192,7168]{1,0:T(8,128)} %convolution_multiply_fusion, bf16[2,512,7168]{2,1,0:T(8,128)(2,1)} %param.11, f32[192]{0:T(256)S(1)} %bitcast.166, f32[192,512]{1,0:T(8,128)S(1)} %fusion.8, bf16[192,7168]{1,0:T(8,128)(2,1)S(1)} %reshape.141, bf16[2,7168,512]{2,1,0:T(8,128)(2,1)} %param.9), kind=kOutput, calls=%fused_computation.3 | convolution fusion | flops 2823290880 | bytes 26084096 | tf_op jit(solution)/shard_map/dot_general | solution.py:69
  106.2 4.6 %reshape.142 = bf16[2,16,6,7168]{3,2,1,0:T(8,128)(2,1)} reshape(bf16[192,7168]{1,0:T(8,128)(2,1)} %fusion.1) | data formatting | bytes 5505024 | tf_op jit(solution)/shard_map/reshape | solution.py:112
  112.7 1.0 fusion.31
  115.6 1.0 fusion.28
  117.5 1.0 fusion.26
  118.5 1.0 fusion.25
  126.2 4.4 %copy.144 = bf16[16,2,1,6,7168]{4,1,3,2,0:T(2,128)(2,1)} copy(bf16[16,2,1,6,7168]{4,3,1,2,0:T(8,128)(2,1)S(1)} %fusion.18) | data formatting | bytes 5505024 | tf_op jit(solution)/shard_map/stack | solution.py:115
  130.5 5.9 %all-to-all-start.2 = ((bf16[16,2,1,6,7168]{4,1,3,2,0:T(2,128)(2,1)}), bf16[16,2,1,6,7168]{4,1,3,2,0:T(2,128)(2,1)S(1)}, u32[]{:S(2)}, u32[]{:S(2)}) async-start(bf16[16,2,1,6,7168]{4,1,3,2,0:T(2,128)(2,1)} %copy.144), calls=%async_computation.2 | async-start | bytes 5505024 | tf_op jit(solution)/shard_map/all_to_all | solution.py:114
  136.9 61.0 %all-to-all-done.2 = bf16[16,2,1,6,7168]{4,1,3,2,0:T(2,128)(2,1)S(1)} async-done(((bf16[16,2,1,6,7168]{4,1,3,2,0:T(2,128)(2,1)}), bf16[16,2,1,6,7168]{4,1,3,2,0:T(2,128)(2,1)S(1)}, u32[]{:S(2)}, u32[]{:S(2)}) %all-to-all-start.2) | async-done | bytes 2752544 | tf_op jit(solution)/shard_map/all_to_all | solution.py:114
  197.9 2.5 %copy.145 = bf16[2,16,1,6,7168]{4,3,1,0,2:T(8,128)(2,1)} copy(bf16[2,16,1,6,7168]{4,0,3,2,1:T(2,128)(2,1)S(1)} %bitcast.160) | data formatting | bytes 5505024 | tf_op jit(solution)/shard_map/reshape | solution.py:113
  200.5 3.2 %reshape_reshape.3 = bf16[192,7168]{1,0:T(8,128)(2,1)S(1)} reshape(bf16[2,16,1,6,7168]{4,3,1,0,2:T(8,128)(2,1)} %copy.145) | data formatting | bytes 5505024 | tf_op jit(solution)/shard_map/reshape;reshape | solution.py:129
  203.7 1.2 convolution_convert_fusion.1
  (70 shorter events, 17.8 us)
Async XLA Ops:
  0.0 2.1 %copy-start = (bf16[12,7168]{1,0:T(8,128)(2,1)S(1)}, bf16[12,7168]{1,0:T(8,128)(2,1)}, u32[]{:S(2)}) copy-start(bf16[12,7168]{1,0:T(8,128)(2,1)} %param.6) | copy-start | bytes 516100
  2.6 8.1 %copy-start.2 = (s32[12,8]{0,1:T(8,128)S(1)}, s32[12,8]{0,1:T(8,128)}, u32[]{:S(2)}) copy-start(s32[12,8]{0,1:T(8,128)} %param.7) | copy-start | bytes 1156
  2.7 8.2 %copy-start.3 = (f32[12,8]{0,1:T(8,128)S(1)}, f32[12,8]{0,1:T(8,128)}, u32[]{:S(2)}) copy-start(f32[12,8]{0,1:T(8,128)} %param.8) | copy-start | bytes 1156
  4.2 48.3 %all-to-all-start.1 = ((bf16[16,6,7168]{2,1,0:T(8,128)(2,1)}), bf16[16,6,7168]{2,1,0:T(8,128)(2,1)S(1)}, u32[]{:S(2)}, u32[]{:S(2)}) async-start(bf16[16,6,7168]{2,1,0:T(8,128)(2,1)} %reshape.140), calls=%async_computation.1 | async-start | bytes 3670016 | tf_op jit(solution)/shard_map/all_to_all | solution.py:85
  54.4 11.8 %collective-permute-start.1 = (bf16[1,16,6,7168]{3,1,2,0:T(8,128)(2,1)}, bf16[1,16,6,7168]{3,1,2,0:T(8,128)(2,1)S(1)}, u32[]{:S(2)}, u32[]{:S(2)}) collective-permute-start(bf16[1,16,6,7168]{3,1,2,0:T(8,128)(2,1)} %copy.126), channel_id=1, source_target_pairs={{0,1},{1,0},{2,3},{3,2},{4,5},{5,4},{6,7},{7,6},{8,9},{9,8},{10,11... | collective-permute-start | bytes 4128776 | tf_op jit(solution)/shard_map/ppermute | solution.py:17
  55.7 8.9 %all-to-all-start = ((bf16[16,6,2]{1,2,0:T(2,128)(2,1)}), bf16[16,6,2]{1,2,0:T(2,128)(2,1)S(1)}, u32[]{:S(2)}, u32[]{:S(2)}) async-start(bf16[16,6,2]{1,2,0:T(2,128)(2,1)} %convolution_convert_fusion.2), calls=%async_computation | async-start | bytes 16384 | tf_op jit(solution)/shard_map/all_to_all | solution.py:86
  64.5 1.5 collective-permute-start
  130.5 67.4 %all-to-all-start.2 = ((bf16[16,2,1,6,7168]{4,1,3,2,0:T(2,128)(2,1)}), bf16[16,2,1,6,7168]{4,1,3,2,0:T(2,128)(2,1)S(1)}, u32[]{:S(2)}, u32[]{:S(2)}) async-start(bf16[16,2,1,6,7168]{4,1,3,2,0:T(2,128)(2,1)} %copy.144), calls=%async_computation.2 | async-start | bytes 5505024 | tf_op jit(solution)/shard_map/all_to_all | solution.py:114
  197.9 7.0 %copy-start.1 = (bf16[12,7168]{1,0:T(8,128)(2,1)S(1)}, bf16[12,7168]{1,0:T(8,128)(2,1)}, u32[]{:S(2)}) copy-start(bf16[12,7168]{1,0:T(8,128)(2,1)} %param.6) | copy-start | bytes 516100
